TPU v7x, 32 devices: a whole 2x2x4 slice. The times are simulated.
32 devices in a mesh: blk: 4 (over y, x), ep: 8 (over z, core).
Axes of the slice: x: 2, y: 2, z: 4, core: 2. Of those that a mesh axis runs over, the one named last changes fastest.
Arguments:
- tokens: bfloat16 [4096, 1024], P(('blk', 'ep')), may hold values from -6 to 6
- expert_ids: int32 [4096, 6], P(('blk', 'ep')), may hold values from 0 to 63, all different within a row; in each aligned block of 128 rows (0 to 127, 128 to 255, ...) at most 16 rows name the same one
- route_weight: float32 [4096, 6], P(('blk', 'ep')), may hold values from 0.05 to 1
- gate_weight: bfloat16 [1024, 64, 768], P('blk', 'ep'), may hold values from -0.1875 to 0.1875
- up_weight: bfloat16 [1024, 64, 768], P('blk', 'ep'), may hold values from -0.1875 to 0.1875
- down_weight: bfloat16 [1024, 64, 768], P('blk', 'ep'), may hold values from -0.21875 to 0.21875
- out_grad: bfloat16 [4096, 1024], P(('blk', 'ep')), may hold values from -6 to 6
Outputs:
- layer_output: bfloat16 [4096, 1024], P(('blk', 'ep'))
- grad_tokens: float32 [4096, 1024], P(('blk', 'ep'))
- grad_route: float32 [4096, 6], P(('blk', 'ep'))
- grad_gate: float32 [1024, 64, 768], P('blk', 'ep')
- grad_up: float32 [1024, 64, 768], P('blk', 'ep')
- grad_down: float32 [1024, 64, 768], P('blk', 'ep')
Inputs may be any that keep to these rules, and one draw needn't show every extreme that they name: `expert_ids`: within the 128 tokens of one device, the 6 experts of a token differ, and no expert is named by more than 16 of them; in every draw some expert is named by exactly 16 tokens of some device.
All inputs are finite; a program needn't handle non-finite values.
Results may differ from a plain program's by a relative error of at most 0.008.
Values may be sent and summed in bfloat16 or wider, within the bound.
No kernel may reach another device: no remote copies, remote signals or barrier semaphores. Data moves between devices by JAX's collectives and lax.ppermute only.
A program may use at most 256 MiB of HBM per device.

v0:
```python
import jax
import jax.numpy as jnp
from jax import lax
from jax.sharding import PartitionSpec as P

EXPERTS = 64
CAP = 16


def expand_rows(routed, weights):
    return jnp.einsum("erd,def->erf", routed, weights, preferred_element_type=jnp.float32)


def contract_rows(inner, weights):
    return jnp.einsum("erf,def->erd", inner, weights, preferred_element_type=jnp.float32)


def outer_rows(routed, inner):
    return jnp.einsum("erd,erf->def", routed, inner, preferred_element_type=jnp.float32)


def body(tokens, expert_ids, route_weight, gate_weight, up_weight, down_weight, out_grad):
    tok_count, model_width = tokens.shape
    top_count = expert_ids.shape[1]
    experts = EXPERTS
    capacity = CAP
    flat_ids = expert_ids.reshape(-1)
    onehot = (flat_ids[:, None] == jnp.arange(experts, dtype=jnp.int32)[None, :]).astype(jnp.int32)
    slot_rank = jnp.sum((jnp.cumsum(onehot, axis=0) - 1) * onehot, axis=1)
    target = flat_ids * capacity + slot_rank
    repeated = jnp.repeat(tokens, top_count, axis=0)
    outgoing = jnp.zeros((experts * capacity, model_width), jnp.bfloat16).at[target].set(repeated)
    received = lax.all_to_all(
        outgoing.reshape(experts, capacity, model_width),
        "ep",
        split_axis=0,
        concat_axis=1,
        tiled=True,
    )
    gate_full, up_full, down_full = (
        lax.all_gather(gate_weight, "blk", axis=0, tiled=True),
        lax.all_gather(up_weight, "blk", axis=0, tiled=True),
        lax.all_gather(down_weight, "blk", axis=0, tiled=True),
    )
    gate_pre = expand_rows(received, gate_full)
    up_pre = expand_rows(received, up_full)
    gate_sig = jax.nn.sigmoid(gate_pre)
    hidden = (gate_pre * gate_sig * up_pre).astype(jnp.bfloat16)
    expert_out = contract_rows(hidden, down_full).astype(jnp.bfloat16)
    returned = lax.all_to_all(expert_out, "ep", split_axis=1, concat_axis=0, tiled=True)
    chosen = returned.reshape(experts * capacity, model_width)[target].reshape(
        tok_count, top_count, model_width
    )
    chosen_f32 = chosen.astype(jnp.float32)
    layer_output = jnp.sum(route_weight[:, :, None] * chosen_f32, axis=1).astype(jnp.bfloat16)
    grad_f32 = out_grad.astype(jnp.float32)
    grad_route = jnp.sum(chosen_f32 * grad_f32[:, None, :], axis=2)
    slot_grad = (route_weight[:, :, None] * grad_f32[:, None, :]).astype(jnp.bfloat16)
    grad_send = (
        jnp.zeros((experts * capacity, model_width), jnp.bfloat16)
        .at[target]
        .set(slot_grad.reshape(-1, model_width))
    )
    grad_recv = lax.all_to_all(
        grad_send.reshape(experts, capacity, model_width),
        "ep",
        split_axis=0,
        concat_axis=1,
        tiled=True,
    )
    down_summed = lax.psum_scatter(
        outer_rows(grad_recv, hidden).astype(jnp.bfloat16), "blk", scatter_dimension=0, tiled=True
    ).astype(jnp.float32)
    grad_hidden = expand_rows(grad_recv, down_full)
    gate_delta = (grad_hidden * up_pre * gate_sig * (1.0 + gate_pre * (1.0 - gate_sig))).astype(
        jnp.bfloat16
    )
    up_delta = (grad_hidden * gate_pre * gate_sig).astype(jnp.bfloat16)
    input_grad = (contract_rows(gate_delta, gate_full) + contract_rows(up_delta, up_full)).astype(
        jnp.bfloat16
    )
    grad_back = lax.all_to_all(input_grad, "ep", split_axis=1, concat_axis=0, tiled=True)
    picked_grad = grad_back.reshape(experts * capacity, model_width)[target].reshape(
        tok_count, top_count, model_width
    )
    grad_tokens = jnp.sum(picked_grad.astype(jnp.float32), axis=1)
    pair_summed = lax.psum_scatter(
        jnp.stack(
            [outer_rows(received, gate_delta), outer_rows(received, up_delta)], axis=1
        ).astype(jnp.bfloat16),
        "blk",
        scatter_dimension=0,
        tiled=True,
    ).astype(jnp.float32)
    grad_gate = pair_summed[:, 0]
    grad_up = pair_summed[:, 1]
    return (layer_output, grad_tokens, grad_route, grad_gate, grad_up, down_summed)


def solution(mesh):
    in_specs = (
        P(("blk", "ep"), None),
        P(("blk", "ep"), None),
        P(("blk", "ep"), None),
        P("blk", "ep", None),
        P("blk", "ep", None),
        P("blk", "ep", None),
        P(("blk", "ep"), None),
    )
    out_specs = (
        P(("blk", "ep"), None),
        P(("blk", "ep"), None),
        P(("blk", "ep"), None),
        P("blk", "ep", None),
        P("blk", "ep", None),
        P("blk", "ep", None),
    )
    return jax.shard_map(body, mesh=mesh, in_specs=in_specs, out_specs=out_specs, check_vma=False)
```

profile of v0, /device:TPU:0, one launch (start us, length us, event | category | flops | bytes accessed | tf_op | source)
XLA Modules:
  0.0 790.4 jit_solution(9528315452976201955)
XLA Ops:
  7.2 4.2 copy.50
  11.5 1.8 copy-done.4
  13.3 2.3 copy.51
  15.6 1.8 copy-done.5
  17.4 2.3 copy.52
  21.1 1.8 reduce-window.6
  25.1 8.0 %scatter_custom_fusion = bf16[1024,1024]{1,0:T(8,128)(2,1)} fusion(s32[768]{0:T(1024)S(1)} %fusion.8, bf16[768,1024]{1,0:T(8,128)(2,1)} %reshape.126, bf16[]{:T(256)} %constant.7.clone.1), kind=kCustom, calls=%fused_computation.22 | custom fusion | bytes 2097664 | tf_op jit(solution)/shard_map/scatter | solution.py:32
  33.1 6.8 all-to-all-start
  40.0 2.5 mul.89
  42.5 3.1 mul.90
  45.9 9.6 %scatter_custom_fusion.1 = bf16[1024,1024]{1,0:T(8,128)(2,1)} fusion(s32[768]{0:T(1024)S(1)} %fusion.8, f32[768,1024]{1,0:T(8,128)S(1)} %mul.90, f32[768]{0:T(1024)S(1)} %mul.87, bf16[]{:T(256)} %constant.7.clone.1), kind=kCustom, calls=%fused_computation.19 | custom fusion | flops 1572864 | bytes 5246978 | tf_op jit(solution)/shard_map/scatter | solution.py:62
  55.5 33.6 %all-to-all-done = bf16[64,16,1024]{2,1,0:T(8,128)(2,1)} async-done(((bf16[64,16,1024]{2,1,0:T(8,128)(2,1)}), bf16[64,16,1024]{2,1,0:T(8,128)(2,1)}, u32[]{:S(2)}, u32[]{:S(2)}) %all-to-all-start) | async-done | bytes 2097184 | tf_op jit(solution)/shard_map/all_to_all | solution.py:33
  89.1 4.4 all-to-all-start.2
  94.0 1.8 copy.49
  95.8 46.7 %all-to-all-done.2 = bf16[64,16,1024]{2,1,0:T(8,128)(2,1)} async-done(((bf16[64,16,1024]{2,1,0:T(8,128)(2,1)}), bf16[64,16,1024]{2,1,0:T(8,128)(2,1)}, u32[]{:S(2)}, u32[]{:S(2)}) %all-to-all-start.2) | async-done | bytes 2097184 | tf_op jit(solution)/shard_map/all_to_all | solution.py:64
  142.5 3.3 copy.56
  145.8 10.2 %fusion.9 = f32[8,128,768]{2,1,0:T(8,128)} fusion(bf16[8,128,1024]{2,1,0:T(8,128)(2,1)S(1)} %bitcast.68, bf16[1024,8,768]{2,0,1:T(8,128)(2,1)} %all-gather.4.cloned.1.call-done), kind=kOutput, calls=%fused_computation.36 | convolution fusion | flops 1610612736 | bytes 17825792 | tf_op jit(solution)/shard_map/erd,def->erf/dot_general | solution.py:11
  156.0 105.8 %all-gather.6.cloned.1.call-done = bf16[1024,8,768]{2,0,1:T(8,128)(2,1)} async-done(((bf16[256,8,768]{2,0,1:T(8,128)(2,1)}), bf16[1024,8,768]{2,0,1:T(8,128)(2,1)}) %all-gather.6.cloned.1.call-update) | async-done | bytes 12582928 | tf_op jit(solution)/shard_map/all_gather | solution.py:42
  261.7 8.1 %fusion.10 = f32[8,128,768]{2,1,0:T(8,128)} fusion(bf16[8,128,1024]{2,1,0:T(8,128)(2,1)S(1)} %bitcast.69, bf16[1024,8,768]{2,0,1:T(8,128)(2,1)} %all-gather.6.cloned.1.call-done), kind=kOutput, calls=%fused_computation.37 | convolution fusion | flops 1610612736 | bytes 17825792 | tf_op jit(solution)/shard_map/erd,def->erf/dot_general | solution.py:11
  269.8 116.3 %all-gather.8.cloned.1.call-done = bf16[1024,8,768]{2,0,1:T(8,128)(2,1)} async-done(((bf16[256,8,768]{2,0,1:T(8,128)(2,1)}), bf16[1024,8,768]{2,0,1:T(8,128)(2,1)}) %all-gather.8.cloned.1.call-update) | async-done | bytes 12582928 | tf_op jit(solution)/shard_map/all_gather | solution.py:43
  386.1 11.7 %multiply_convert_fusion = (bf16[8,128,768]{2,1,0:T(8,128)(2,1)}, bf16[8,128,768]{2,1,0:T(8,128)(2,1)}, bf16[8,128,768]{2,1,0:T(8,128)(2,1)S(1)}) fusion(f32[8,128,768]{2,1,0:T(8,128)} %fusion.9, f32[8,128,768]{2,1,0:T(8,128)} %fusion.10, bf16[8,128,1024]{2,1,0:T(8,128)(2,1)} %bitcast.73, bf16[1024,8,768]{2,0,1:T(8,128)(2,1)} %all-gather.8.cloned.1.call-done), kind=kOutput, calls=%fused_computation.13 | convolution fusion | flops 1623195648 | bytes 25690112 | tf_op jit(solution)/shard_map/erd,def->erf/dot_general | solution.py:11
  399.0 6.3 convert_bitcast_fusion
  405.5 8.4 %convert_bitcast_fusion.1 = bf16[1024,1,8,768]{0,3,2,1:T(8,128)(2,1)} fusion(bf16[8,128,768]{2,1,0:T(8,128)(2,1)} %get-tuple-element.28, bf16[8,128,1024]{2,1,0:T(8,128)(2,1)S(1)} %bitcast.70), kind=kOutput, calls=%fused_computation.6 | convolution fusion | flops 1616904192 | bytes 16252928 | tf_op jit(solution)/shard_map/erd,erf->def/dot_general | solution.py:19
  413.9 6.6 convert_bitcast_fusion.2
  420.5 21.0 %pad_maximum_fusion = bf16[1024,2,8,768]{0,3,2,1:T(8,128)(2,1)} fusion(bf16[1024,1,8,768]{0,3,2,1:T(8,128)(2,1)} %convert_bitcast_fusion.1, bf16[1024,1,8,768]{0,3,2,1:T(8,128)(2,1)} %convert_bitcast_fusion.2), kind=kLoop, calls=%fused_computation.4 | loop fusion | flops 12582912 | bytes 50331648 | tf_op jit(solution)/shard_map/stack | solution.py:88
  442.9 9.1 %convolution_convert_fusion = bf16[8,128,1024]{2,1,0:T(8,128)(2,1)S(1)} fusion(bf16[8,128,768]{2,1,0:T(8,128)(2,1)S(1)} %copy-done.3, bf16[1024,8,768]{2,0,1:T(8,128)(2,1)} %all-gather.8.cloned.1.call-done), kind=kOutput, calls=%fused_computation.18 | convolution fusion | flops 1611661312 | bytes 16252928 | tf_op jit(solution)/shard_map/erf,def->erd/dot_general | solution.py:15
  452.0 2.5 copy.53
  454.5 4.6 all-to-all-start.1
  459.1 9.5 %fusion.11 = f32[8,128,1024]{2,1,0:T(8,128)S(1)} fusion(bf16[8,128,768]{2,1,0:T(8,128)(2,1)} %get-tuple-element.29, bf16[1024,8,768]{2,0,1:T(8,128)(2,1)} %all-gather.4.cloned.1.call-done), kind=kOutput, calls=%fused_computation.38 | convolution fusion | flops 1610612736 | bytes 18350080 | tf_op jit(solution)/shard_map/erf,def->erd/dot_general | solution.py:15
  468.6 10.7 %add_convert_fusion = bf16[8,128,1024]{2,1,0:T(8,128)(2,1)} fusion(f32[8,128,1024]{2,1,0:T(8,128)S(1)} %fusion.11, bf16[8,128,768]{2,1,0:T(8,128)(2,1)} %get-tuple-element.28, bf16[1024,8,768]{2,0,1:T(8,128)(2,1)} %all-gather.6.cloned.1.call-done), kind=kOutput, calls=%fused_computation.11 | convolution fusion | flops 1612709888 | bytes 20447232 | tf_op jit(solution)/shard_map/erf,def->erd/dot_general | solution.py:15
  479.3 4.1 copy.57
  483.3 24.9 %all-to-all-done.1 = bf16[8,128,1024]{2,0,1:T(8,128)(2,1)} async-done(((bf16[8,128,1024]{2,0,1:T(8,128)(2,1)}), bf16[8,128,1024]{2,0,1:T(8,128)(2,1)}, u32[]{:S(2)}, u32[]{:S(2)}) %all-to-all-start.1) | async-done | bytes 2097184 | tf_op jit(solution)/shard_map/all_to_all | solution.py:50
  508.2 4.6 all-to-all-start.3
  512.9 2.9 copy.54
  515.8 3.6 gather_fusion
  519.3 4.0 reshape.104
  523.3 38.6 %all-to-all-done.3 = bf16[8,128,1024]{2,0,1:T(8,128)(2,1)} async-done(((bf16[8,128,1024]{2,0,1:T(8,128)(2,1)}), bf16[8,128,1024]{2,0,1:T(8,128)(2,1)}, u32[]{:S(2)}, u32[]{:S(2)}) %all-to-all-start.3) | async-done | bytes 2097184 | tf_op jit(solution)/shard_map/all_to_all | solution.py:82
  561.9 2.8 copy.58
  564.7 3.6 gather_fusion.1
  568.2 3.9 reshape.105
  572.2 5.2 multiply_reduce_fusion
  578.0 4.3 reduce_sum.41
  582.3 5.7 copy.65
  588.0 163.0 %reduce-scatter.3.cloned.1.call-done = bf16[256,2,8,768]{0,3,2,1:T(8,128)(2,1)} async-done(((bf16[1024,2,8,768]{0,3,2,1:T(8,128)(2,1)}), bf16[256,2,8,768]{0,3,2,1:T(8,128)(2,1)}) %reduce-scatter.3.cloned.1.call-update) | async-done | bytes 6291472 | tf_op jit(solution)/shard_map/reduce_scatter | solution.py:87
  751.0 8.7 %convert_element_type.72 = f32[256,2,8,768]{0,3,2,1:T(8,128)} convert(bf16[256,2,8,768]{0,3,2,1:T(8,128)(2,1)} %reduce-scatter.3.cloned.1.call-done) | non-fusion elementwise | flops 3145728 | bytes 18874368 | tf_op jit(solution)/shard_map/convert_element_type | solution.py:94
  759.7 10.5 %slice_bitcast_fusion = (f32[256,8,768]{0,2,1:T(8,128)}, f32[256,8,768]{0,2,1:T(8,128)}) fusion(f32[256,2,8,768]{0,3,2,1:T(8,128)} %convert_element_type.72), kind=kLoop, calls=%fused_computation.8 | loop fusion | bytes 25165824 | tf_op jit(solution)/shard_map/squeeze | solution.py:96
  770.2 6.7 copy.63
  776.9 6.7 copy.64
  (48 shorter events, 8.0 us)
Async XLA Ops:
  7.2 138.6 %all-gather.4.cloned.1.call-start = ((), (), s32[]{:S(2)}) async-start(), calls=%async_computation.6 | async-start | bytes 15728640 | tf_op jit(solution)/shard_map/all_gather | solution.py:41
  11.4 1.9 copy-start.4
  11.4 250.3 %all-gather.6.cloned.1.call-start = ((), (), s32[]{:S(2)}) async-start(), calls=%async_computation.7 | async-start | bytes 15728640 | tf_op jit(solution)/shard_map/all_gather | solution.py:42
  15.5 1.9 copy-start.5
  15.6 370.6 %all-gather.8.cloned.1.call-start = ((), (), s32[]{:S(2)}) async-start(), calls=%async_computation.8 | async-start | bytes 15728640 | tf_op jit(solution)/shard_map/all_gather | solution.py:43
  19.7 0.7 copy-start.8
  19.7 3.5 copy-start.7
  25.1 14.9 %copy-start.6 = (bf16[128,1024]{1,0:T(8,128)(2,1)S(1)}, bf16[128,1024]{1,0:T(8,128)(2,1)}, u32[]{:S(2)}) copy-start(bf16[128,1024]{1,0:T(8,128)(2,1)} %param.13) | copy-start | bytes 786436
  33.1 56.0 %all-to-all-start = ((bf16[64,16,1024]{2,1,0:T(8,128)(2,1)}), bf16[64,16,1024]{2,1,0:T(8,128)(2,1)}, u32[]{:S(2)}, u32[]{:S(2)}) async-start(bf16[64,16,1024]{2,1,0:T(8,128)(2,1)} %bitcast.1), calls=%async_computation | async-start | bytes 4194304 | tf_op jit(solution)/shard_map/all_to_all | solution.py:33
  42.5 3.1 copy-start.9
  89.1 53.4 %all-to-all-start.2 = ((bf16[64,16,1024]{2,1,0:T(8,128)(2,1)}), bf16[64,16,1024]{2,1,0:T(8,128)(2,1)}, u32[]{:S(2)}, u32[]{:S(2)}) async-start(bf16[64,16,1024]{2,1,0:T(8,128)(2,1)} %bitcast.72), calls=%async_computation.2 | async-start | bytes 4194304 | tf_op jit(solution)/shard_map/all_to_all | solution.py:64
  93.5 488.8 %reduce-scatter.5.cloned.1.call-start = ((), (), s32[]{:S(2)}) async-start(), calls=%async_computation.10 | async-start | bytes 15728640 | tf_op jit(solution)/shard_map/reduce_scatter | solution.py:71
  386.1 12.8 %copy-start = (bf16[8,8,16,1024]{3,2,1,0:T(8,128)(2,1)S(1)}, bf16[8,8,16,1024]{3,2,1,0:T(8,128)(2,1)}, u32[]{:S(2)}) copy-start(bf16[8,8,16,1024]{3,2,1,0:T(8,128)(2,1)} %copy.56) | copy-start | bytes 6291460
  397.8 1.1 copy-start.2
  405.3 345.7 %reduce-scatter.3.cloned.1.call-start = ((), (), s32[]{:S(2)}) async-start(), calls=%async_computation.9 | async-start | bytes 31457280 | tf_op jit(solution)/shard_map/reduce_scatter | solution.py:87
  405.5 8.4 %copy-start.1 = (bf16[8,128,768]{2,1,0:T(8,128)(2,1)S(1)}, bf16[8,128,768]{2,1,0:T(8,128)(2,1)}, u32[]{:S(2)}) copy-start(bf16[8,128,768]{2,1,0:T(8,128)(2,1)} %get-tuple-element.29) | copy-start | bytes 4718596
  441.4 1.4 copy-start.3
  454.5 53.8 %all-to-all-start.1 = ((bf16[8,128,1024]{2,0,1:T(8,128)(2,1)}), bf16[8,128,1024]{2,0,1:T(8,128)(2,1)}, u32[]{:S(2)}, u32[]{:S(2)}) async-start(bf16[8,128,1024]{2,0,1:T(8,128)(2,1)} %copy.53), calls=%async_computation.1 | async-start | bytes 4194304 | tf_op jit(solution)/shard_map/all_to_all | solution.py:50
  508.2 53.6 %all-to-all-start.3 = ((bf16[8,128,1024]{2,0,1:T(8,128)(2,1)}), bf16[8,128,1024]{2,0,1:T(8,128)(2,1)}, u32[]{:S(2)}, u32[]{:S(2)}) async-start(bf16[8,128,1024]{2,0,1:T(8,128)(2,1)} %copy.57), calls=%async_computation.3 | async-start | bytes 4194304 | tf_op jit(solution)/shard_map/all_to_all | solution.py:82
Sparse Core Ops, SparseCore 0:
  11.5 125.2 all-gather.3
  139.2 122.5 all-gather.5
  263.6 122.5 all-gather.7
  405.4 120.7 reduce-scatter.4
  529.1 221.8 reduce-scatter.2
where the time goes:
time: 797 us; the launch traced here: 790 us
  waiting for transfers between devices  529 us (66%)
  local copies, waits for them, and re-layouts  94.6 us (12%)
  matrix products  80.5 us (10%)
  other arithmetic  50.8 us (6%)
  starting transfers between devices  21.3 us (3%)
  between operations  14.2 us (2%)
    reduce_scatter x1, waiting for transfers between devices, body(): lax.psum_scatter(jnp.stack([outer_rows(received, gate_delta), outer_rows(...  163 us
    all_gather x1, waiting for transfers between devices, body(): lax.all_gather(down_weight, 'blk', axis=0, tiled=True)  116 us
    all_gather x1, waiting for transfers between devices, body(): lax.all_gather(up_weight, 'blk', axis=0, tiled=True)  106 us
    all_to_all x1, waiting for transfers between devices, body(): lax.all_to_all(grad_send.reshape(experts, capacity, model_width), 'ep', s...  46.7 us
    all_to_all x1, waiting for transfers between devices, body(): lax.all_to_all(input_grad, 'ep', split_axis=1, concat_axis=0, tiled=True)  38.6 us
    unnamed x29, local copies, waits for them, and re-layouts  35.5 us
    all_to_all x1, waiting for transfers between devices, body(): lax.all_to_all(outgoing.reshape(experts, capacity, model_width), 'ep', sp...  33.6 us
    dot_general x3, matrix products, expand_rows(): jnp.einsum('erd,def->erf', routed, weights, preferred_element_type=jnp.fl...  29.9 us
  transfers between devices with their start and end apart: 9, of which 7 were waited for; matrix products, arithmetic and copies ran while one was open for 21% of the time, Pallas kernels for 0%

commit v1 on v0

--- a/solution.py
+++ b/solution.py
@@ -5,6 +5,22 @@
 
 EXPERTS = 64
 CAP = 16
+
+
+def collect(x, axis, dim):
+    ways, here, turn = (lax.axis_size(axis), lax.axis_index(axis), x.shape[dim])
+    shape = [n * ways if d == dim else n for d, n in enumerate(x.shape)]
+    full = lax.dynamic_update_slice_in_dim(jnp.zeros(shape, x.dtype), x, here * turn, axis=dim)
+    going_up = going_down = x
+    for far in range(1, ways // 2 + 1):
+        going_up = lax.ppermute(going_up, axis, [(d, (d + 1) % ways) for d in range(ways)])
+        full = lax.dynamic_update_slice_in_dim(full, going_up, (here - far) % ways * turn, axis=dim)
+        if 2 * far < ways:
+            going_down = lax.ppermute(going_down, axis, [(d, (d - 1) % ways) for d in range(ways)])
+            full = lax.dynamic_update_slice_in_dim(
+                full, going_down, (here + far) % ways * turn, axis=dim
+            )
+    return full
 
 
 def expand_rows(routed, weights):
@@ -39,7 +55,7 @@
     )
     gate_full, up_full, down_full = (
         lax.all_gather(gate_weight, "blk", axis=0, tiled=True),
-        lax.all_gather(up_weight, "blk", axis=0, tiled=True),
+        collect(up_weight, "blk", 0),
         lax.all_gather(down_weight, "blk", axis=0, tiled=True),
     )
     gate_pre = expand_rows(received, gate_full)

time: 797 us -> 850 us (1.066)
  waiting for transfers between devices: 529 us -> 562 us
  local copies, waits for them, and re-layouts: 94.6 us -> 116 us
    ppermute x0 -> x3, waiting for transfers between devices: none -> 298 us  [the longest x2 194 us: collect(): lax.ppermute(going_up, axis, [(d, (d + 1) % ways) for d in range(ways)])]
    all_gather x1, waiting for transfers between devices: 116 us -> 0.01 us  [body(): lax.all_gather(down_weight, 'blk', axis=0, tiled=True)]
    all_gather x1 -> x0, waiting for transfers between devices: 106 us -> none  [body(): lax.all_gather(up_weight, 'blk', axis=0, tiled=True)]
    all_to_all x1, waiting for transfers between devices: 33.6 us -> 0.01 us  [body(): lax.all_to_all(outgoing.reshape(experts, capacity, model_width), 'ep', sp...]
    dynamic_update_slice x0 -> x4, local copies, waits for them, and re-layouts: none -> 16.7 us  [the longest x2 8.35 us: collect(): lax.dynamic_update_slice_in_dim(full, going_up, (here - far) % ways * tur...]
    all_to_all x1, waiting for transfers between devices: 46.7 us -> 37.7 us  [body(): lax.all_to_all(grad_send.reshape(experts, capacity, model_width), 'ep', s...]
    unnamed x29 -> x32, local copies, waits for them, and re-layouts: 35.5 us -> 33.9 us
  transfers between devices with their start and end apart: 9 -> 11, of which waited for: 7 -> 8; matrix products, arithmetic and copies ran while one was open for 21% -> 21% of each run, Pallas kernels for 0% -> 0%
where the time goes in v1:
time: 850 us; the launch traced here: 840 us
  waiting for transfers between devices  562 us (66%)
  local copies, waits for them, and re-layouts  116 us (14%)
  matrix products  73.9 us (9%)
  other arithmetic  50.5 us (6%)
  starting transfers between devices  23.4 us (3%)
  between operations  14.4 us (2%)
    ppermute x2, waiting for transfers between devices, collect(): lax.ppermute(going_up, axis, [(d, (d + 1) % ways) for d in range(ways)])  194 us
    reduce_scatter x1, waiting for transfers between devices, body(): lax.psum_scatter(jnp.stack([outer_rows(received, gate_delta), outer_rows(...  162 us
    ppermute x1, waiting for transfers between devices, collect(): lax.ppermute(going_down, axis, [(d, (d - 1) % ways) for d in range(ways)])  104 us
    all_to_all x1, waiting for transfers between devices, body(): lax.all_to_all(input_grad, 'ep', split_axis=1, concat_axis=0, tiled=True)  38.7 us
    all_to_all x1, waiting for transfers between devices, body(): lax.all_to_all(grad_send.reshape(experts, capacity, model_width), 'ep', s...  37.7 us
    unnamed x32, local copies, waits for them, and re-layouts  33.9 us
    dot_general x3, matrix products, contract_rows(): jnp.einsum('erf,def->erd', inner, weights, preferred_element_type=jnp.flo...  29.3 us
    all_to_all x1, waiting for transfers between devices, body(): lax.all_to_all(expert_out, 'ep', split_axis=1, concat_axis=0, tiled=True)  24.9 us
  transfers between devices with their start and end apart: 11, of which 8 were waited for; matrix products, arithmetic and copies ran while one was open for 21% of the time, Pallas kernels for 0%

profile of v1, /device:TPU:0, one launch (start us, length us, event | category | flops | bytes accessed | tf_op | source)
XLA Modules:
  0.0 840.4 jit_solution(14204788488905423617)
XLA Ops:
  7.2 4.2 copy.61
  19.0 2.9 mul.105
  21.9 3.7 mul.106
  26.0 9.6 %scatter_custom_fusion.1 = bf16[1024,1024]{1,0:T(8,128)(2,1)} fusion(s32[768]{0:T(1024)S(1)} %fusion.8, f32[768,1024]{1,0:T(8,128)S(1)} %mul.106, f32[768]{0:T(1024)S(1)} %mul.103, bf16[]{:T(256)} %constant.42.clone.1), kind=kCustom, calls=%fused_computation.23 | custom fusion | flops 1572864 | bytes 5246978 | tf_op jit(solution)/shard_map/scatter | solution.py:78
  35.6 6.3 all-to-all-start.2
  45.2 8.2 scatter_custom_fusion
  53.4 37.7 %all-to-all-done.2 = bf16[64,16,1024]{2,1,0:T(8,128)(2,1)} async-done(((bf16[64,16,1024]{2,1,0:T(8,128)(2,1)}), bf16[64,16,1024]{2,1,0:T(8,128)(2,1)}, u32[]{:S(2)}, u32[]{:S(2)}) %all-to-all-start.2) | async-done | bytes 2097184 | tf_op jit(solution)/shard_map/all_to_all | solution.py:80
  91.1 3.6 all-to-all-start
  94.8 2.5 collective-permute-start.1
  97.3 76.7 %collective-permute-done = bf16[256,8,768]{2,1,0:T(8,128)(2,1)} collective-permute-done((bf16[256,8,768]{2,1,0:T(8,128)(2,1)}, bf16[256,8,768]{2,1,0:T(8,128)(2,1)}, u32[]{:S(2)}, u32[]{:S(2)}) %collective-permute-start) | collective-permute-done | bytes 3145760 | tf_op jit(solution)/shard_map/ppermute | solution.py:16
  173.9 5.4 broadcast_in_dim.5
  179.3 4.2 copy_dynamic-update-slice_fusion.3
  183.5 4.2 copy_dynamic-update-slice_fusion.2
  187.7 104.2 %collective-permute-done.1 = bf16[256,8,768]{2,1,0:T(8,128)(2,1)} collective-permute-done((bf16[256,8,768]{2,1,0:T(8,128)(2,1)}, bf16[256,8,768]{2,1,0:T(8,128)(2,1)}, u32[]{:S(2)}, u32[]{:S(2)}) %collective-permute-start.1) | collective-permute-done | bytes 3145760 | tf_op jit(solution)/shard_map/ppermute | solution.py:19
  291.9 4.2 copy_dynamic-update-slice_fusion.1
  296.1 3.2 copy.65
  302.4 117.3 %collective-permute-done.2 = bf16[256,8,768]{2,1,0:T(8,128)(2,1)} collective-permute-done((bf16[256,8,768]{2,1,0:T(8,128)(2,1)}, bf16[256,8,768]{2,1,0:T(8,128)(2,1)}, u32[]{:S(2)}, u32[]{:S(2)}) %collective-permute-start.2) | collective-permute-done | bytes 3145760 | tf_op jit(solution)/shard_map/ppermute | solution.py:16
  419.8 4.2 copy_dynamic-update-slice_fusion
  423.9 8.7 %fusion.10 = f32[8,128,768]{2,1,0:T(8,128)} fusion(bf16[8,128,1024]{2,1,0:T(8,128)(2,1)} %bitcast.72, bf16[1024,8,768]{2,0,1:T(8,128)(2,1)} %all-gather.5.cloned.1.call-done), kind=kOutput, calls=%fused_computation.41 | convolution fusion | flops 1610612736 | bytes 17825792 | tf_op jit(solution)/shard_map/erd,def->erf/dot_general | solution.py:27
  433.0 8.2 fusion.9
  442.3 6.3 multiply_convert_fusion
  449.8 6.3 convert_bitcast_fusion
  456.4 8.4 convert_bitcast_fusion.1
  464.8 6.5 convert_bitcast_fusion.2
  471.3 21.0 %pad_maximum_fusion = bf16[1024,2,8,768]{0,3,2,1:T(8,128)(2,1)} fusion(bf16[1024,1,8,768]{0,3,2,1:T(8,128)(2,1)} %convert_bitcast_fusion.1, bf16[1024,1,8,768]{0,3,2,1:T(8,128)(2,1)} %convert_bitcast_fusion.2), kind=kLoop, calls=%fused_computation.4 | loop fusion | flops 12582912 | bytes 50331648 | tf_op jit(solution)/shard_map/stack | solution.py:104
  493.7 9.1 %convolution_convert_fusion = bf16[8,128,1024]{2,1,0:T(8,128)(2,1)S(1)} fusion(bf16[8,128,768]{2,1,0:T(8,128)(2,1)S(1)} %copy-done.5, bf16[1024,8,768]{2,0,1:T(8,128)(2,1)} %all-gather.5.cloned.1.call-done), kind=kOutput, calls=%fused_computation.22 | convolution fusion | flops 1611661312 | bytes 16252928 | tf_op jit(solution)/shard_map/erf,def->erd/dot_general | solution.py:31
  502.9 2.5 copy.62
  505.3 4.5 all-to-all-start.1
  509.8 9.5 %fusion.11 = f32[8,128,1024]{2,1,0:T(8,128)S(1)} fusion(bf16[8,128,768]{2,1,0:T(8,128)(2,1)} %get-tuple-element.29, bf16[1024,8,768]{2,0,1:T(8,128)(2,1)} %all-gather.3.cloned.1.call-done), kind=kOutput, calls=%fused_computation.42 | convolution fusion | flops 1610612736 | bytes 18350080 | tf_op jit(solution)/shard_map/erf,def->erd/dot_general | solution.py:31
  519.4 10.7 %add_convert_fusion = bf16[8,128,1024]{2,1,0:T(8,128)(2,1)} fusion(f32[8,128,1024]{2,1,0:T(8,128)S(1)} %fusion.11, bf16[8,128,768]{2,1,0:T(8,128)(2,1)} %get-tuple-element.28, bf16[1024,8,768]{2,0,1:T(8,128)(2,1)} %copy_dynamic-update-slice_fusion), kind=kOutput, calls=%fused_computation.11 | convolution fusion | flops 1612709888 | bytes 20447232 | tf_op jit(solution)/shard_map/erf,def->erd/dot_general | solution.py:31
  530.1 4.1 copy.66
  534.1 24.9 %all-to-all-done.1 = bf16[8,128,1024]{2,0,1:T(8,128)(2,1)} async-done(((bf16[8,128,1024]{2,0,1:T(8,128)(2,1)}), bf16[8,128,1024]{2,0,1:T(8,128)(2,1)}, u32[]{:S(2)}, u32[]{:S(2)}) %all-to-all-start.1) | async-done | bytes 2097184 | tf_op jit(solution)/shard_map/all_to_all | solution.py:66
  559.0 4.6 all-to-all-start.3
  563.7 2.8 copy.63
  566.5 3.6 gather_fusion
  570.0 3.9 reshape.104
  573.9 38.7 %all-to-all-done.3 = bf16[8,128,1024]{2,0,1:T(8,128)(2,1)} async-done(((bf16[8,128,1024]{2,0,1:T(8,128)(2,1)}), bf16[8,128,1024]{2,0,1:T(8,128)(2,1)}, u32[]{:S(2)}, u32[]{:S(2)}) %all-to-all-start.3) | async-done | bytes 2097184 | tf_op jit(solution)/shard_map/all_to_all | solution.py:98
  612.7 2.8 copy.67
  615.5 3.6 gather_fusion.1
  619.0 3.9 reshape.105
  622.9 4.9 multiply_reduce_fusion
  628.5 4.3 reduce_sum.41
  632.8 5.8 copy.74
  638.6 162.3 %reduce-scatter.3.cloned.1.call-done = bf16[256,2,8,768]{0,3,2,1:T(8,128)(2,1)} async-done(((bf16[1024,2,8,768]{0,3,2,1:T(8,128)(2,1)}), bf16[256,2,8,768]{0,3,2,1:T(8,128)(2,1)}) %reduce-scatter.3.cloned.1.call-update) | async-done | bytes 6291472 | tf_op jit(solution)/shard_map/reduce_scatter | solution.py:103
  800.8 8.7 %convert_element_type.72 = f32[256,2,8,768]{0,3,2,1:T(8,128)} convert(bf16[256,2,8,768]{0,3,2,1:T(8,128)(2,1)} %reduce-scatter.3.cloned.1.call-done) | non-fusion elementwise | flops 3145728 | bytes 18874368 | tf_op jit(solution)/shard_map/convert_element_type | solution.py:110
  809.5 10.5 %slice_bitcast_fusion = (f32[256,8,768]{0,2,1:T(8,128)}, f32[256,8,768]{0,2,1:T(8,128)}) fusion(f32[256,2,8,768]{0,3,2,1:T(8,128)} %convert_element_type.72), kind=kLoop, calls=%fused_computation.8 | loop fusion | bytes 25165824 | tf_op jit(solution)/shard_map/squeeze | solution.py:112
  820.0 6.7 copy.72
  826.7 6.7 copy.73
  (59 shorter events, 19.4 us)
Async XLA Ops:
  7.2 416.8 %all-gather.5.cloned.1.call-start = ((), (), s32[]{:S(2)}) async-start(), calls=%async_computation.7 | async-start | bytes 15728640 | tf_op jit(solution)/shard_map/all_gather | solution.py:59
  11.4 1.9 copy-start.6
  11.4 421.6 %all-gather.3.cloned.1.call-start = ((), (), s32[]{:S(2)}) async-start(), calls=%async_computation.6 | async-start | bytes 15728640 | tf_op jit(solution)/shard_map/all_gather | solution.py:57
  15.5 0.7 copy-start.10
  15.5 3.5 copy-start.7
  21.9 3.7 copy-start.11
  35.6 7.8 copy-start.9
  35.6 55.5 %all-to-all-start.2 = ((bf16[64,16,1024]{2,1,0:T(8,128)(2,1)}), bf16[64,16,1024]{2,1,0:T(8,128)(2,1)}, u32[]{:S(2)}, u32[]{:S(2)}) async-start(bf16[64,16,1024]{2,1,0:T(8,128)(2,1)} %bitcast.75), calls=%async_computation.2 | async-start | bytes 4194304 | tf_op jit(solution)/shard_map/all_to_all | solution.py:80
  42.0 132.0 %collective-permute-start = (bf16[256,8,768]{2,1,0:T(8,128)(2,1)}, bf16[256,8,768]{2,1,0:T(8,128)(2,1)}, u32[]{:S(2)}, u32[]{:S(2)}) collective-permute-start(bf16[256,8,768]{2,1,0:T(8,128)(2,1)} %param.11), channel_id=1, source_target_pairs={{0,8},{8,16},{16,24},{24,0},{1,9},{9,17},{17,25},{25,1},{2,10},{10... | collective-permute-start | bytes 9437192 | tf_op jit(solution)/shard_map/ppermute | solution.py:16
  91.1 208.2 %all-to-all-start = ((bf16[64,16,1024]{2,1,0:T(8,128)(2,1)}), bf16[64,16,1024]{2,1,0:T(8,128)(2,1)S(1)}, u32[]{:S(2)}, u32[]{:S(2)}) async-start(bf16[64,16,1024]{2,1,0:T(8,128)(2,1)} %bitcast.1), calls=%async_computation | async-start | bytes 4194304 | tf_op jit(solution)/shard_map/all_to_all | solution.py:49
  94.7 538.1 %reduce-scatter.5.cloned.1.call-start = ((), (), s32[]{:S(2)}) async-start(), calls=%async_computation.9 | async-start | bytes 15728640 | tf_op jit(solution)/shard_map/reduce_scatter | solution.py:87
  94.8 197.1 %collective-permute-start.1 = (bf16[256,8,768]{2,1,0:T(8,128)(2,1)}, bf16[256,8,768]{2,1,0:T(8,128)(2,1)}, u32[]{:S(2)}, u32[]{:S(2)}) collective-permute-start(bf16[256,8,768]{2,1,0:T(8,128)(2,1)} %param.11), channel_id=1, source_target_pairs={{0,24},{8,0},{16,8},{24,16},{1,25},{9,1},{17,9},{25,17},{2,26},{10... | collective-permute-start | bytes 9437192 | tf_op jit(solution)/shard_map/ppermute | solution.py:19
  173.9 245.8 %collective-permute-start.2 = (bf16[256,8,768]{2,1,0:T(8,128)(2,1)}, bf16[256,8,768]{2,1,0:T(8,128)(2,1)}, u32[]{:S(2)}, u32[]{:S(2)}) collective-permute-start(bf16[256,8,768]{2,1,0:T(8,128)(2,1)} %collective-permute-done), channel_id=1, source_target_pairs={{0,8},{8,16},{16,24},{24,0},{1,9},{9,17},{17,25},{25,1},{2,10},{10... | collective-permute-start | bytes 9437192 | tf_op jit(solution)/shard_map/ppermute | solution.py:16
  299.3 1.3 copy-start.2
  433.0 9.3 %copy-start = (bf16[1024,8,768]{2,0,1:T(8,128)(2,1)S(1)}, bf16[1024,8,768]{2,0,1:T(8,128)(2,1)}, u32[]{:S(2)}) copy-start(bf16[1024,8,768]{2,0,1:T(8,128)(2,1)} %copy_dynamic-update-slice_fusion) | copy-start | bytes 37748740
  442.3 7.5 copy-start.1
  448.6 1.1 copy-start.4
  456.1 344.7 %reduce-scatter.3.cloned.1.call-start = ((), (), s32[]{:S(2)}) async-start(), calls=%async_computation.8 | async-start | bytes 31457280 | tf_op jit(solution)/shard_map/reduce_scatter | solution.py:103
  456.4 8.4 %copy-start.3 = (bf16[8,128,768]{2,1,0:T(8,128)(2,1)S(1)}, bf16[8,128,768]{2,1,0:T(8,128)(2,1)}, u32[]{:S(2)}) copy-start(bf16[8,128,768]{2,1,0:T(8,128)(2,1)} %get-tuple-element.29) | copy-start | bytes 4718596
  492.3 1.4 copy-start.5
  505.3 53.7 %all-to-all-start.1 = ((bf16[8,128,1024]{2,0,1:T(8,128)(2,1)}), bf16[8,128,1024]{2,0,1:T(8,128)(2,1)}, u32[]{:S(2)}, u32[]{:S(2)}) async-start(bf16[8,128,1024]{2,0,1:T(8,128)(2,1)} %copy.62), calls=%async_computation.1 | async-start | bytes 4194304 | tf_op jit(solution)/shard_map/all_to_all | solution.py:66
  534.1 29.5 %copy-start.8 = (bf16[128,1024]{1,0:T(8,128)(2,1)S(1)}, bf16[128,1024]{1,0:T(8,128)(2,1)}, u32[]{:S(2)}) copy-start(bf16[128,1024]{1,0:T(8,128)(2,1)} %param.13) | copy-start | bytes 786436
  559.0 53.7 %all-to-all-start.3 = ((bf16[8,128,1024]{2,0,1:T(8,128)(2,1)}), bf16[8,128,1024]{2,0,1:T(8,128)(2,1)}, u32[]{:S(2)}, u32[]{:S(2)}) async-start(bf16[8,128,1024]{2,0,1:T(8,128)(2,1)} %copy.66), calls=%async_computation.3 | async-start | bytes 4194304 | tf_op jit(solution)/shard_map/all_to_all | solution.py:98
Sparse Core Ops, SparseCore 0:
  11.5 207.8 all-gather.4
  221.8 211.1 all-gather.2
  456.2 119.7 reduce-scatter.4
  579.0 221.8 reduce-scatter.2
